TPU v7x, 32 devices: a whole 2x2x4 slice. The times are simulated.
32 devices in a mesh: mesh: 8 (over y, x, core), band: 4 (over z).
Axes of the slice: x: 2, y: 2, z: 4, core: 2. Of those that a mesh axis runs over, the one named last changes fastest.
Arguments:
- states: float32 [2, 64, 8192], P(None, 'band', 'mesh'), may hold values from -6 to 6
- frozen: float32 [2, 32, 8192], P(None, 'band', 'mesh'), may hold values from -0.125 to 0.125
- weights: float32 [8, 8192], P(None, 'mesh'), may hold values from 0.1 to 1
- potential: float32 [8192], P('mesh'), may hold values from -2 to 2
- send_list: int32 [8, 8, 256], P('mesh'), may hold values from 0 to 1023
- neighbours: int32 [8, 8192], P(None, 'mesh'), may hold values from 0 to 3071, as said below
Outputs:
- evolved: float32 [2, 64, 8192], P(None, 'band', 'mesh')
Inputs may be any that keep to these rules, and one draw needn't show every extreme that they name: `neighbours`: an entry below 1024 names a point of the same part; an entry 1024 + s * 256 + c names ghost slot c from part s, where part s is at most 3 parts away in the cyclic order of parts or exactly half the number of parts away, and every part names ghost slots from all those parts. Slots of send_list[s, i] that part i never names hold arbitrary points of part s.
All inputs are finite; a program needn't handle non-finite values.
Results may differ from a plain program's by a relative error of at most 0.0001.
Values sent between devices are 32-bit elements; how exact they have to be, the bound alone decides.
No kernel may reach another device: no remote copies, remote signals or barrier semaphores. Data moves between devices by JAX's collectives and lax.ppermute only.
A program may use at most 128 MiB of HBM per device.

v0:
```python
import jax
import jax.numpy as jnp
from jax import lax
from jax.sharding import PartitionSpec as P

NBRS = 8
TERMS = 4
time_step = 0.3


def rotate(field):
    return jnp.stack([field[1], -field[0]])


def body(states, frozen, weights, potential, send_list, neighbours):
    parts = lax.axis_size("mesh")
    rows = states.shape[1]
    capacity = send_list.shape[2]
    routes = send_list[0]
    full_frozen = lax.all_gather(frozen, "band", axis=1, tiled=True)
    total = states
    term = states
    for order in range(1, TERMS + 1):
        paired = jnp.stack([term, rotate(term)])
        partial_intersection = jnp.einsum(
            "cmp,ocjp->omj", full_frozen, paired, precision=lax.Precision.HIGHEST
        )
        intersection = lax.psum(partial_intersection, "mesh")
        packed = jnp.take(term, routes.reshape(-1), axis=2).reshape(2, rows, parts, capacity)
        arrived = lax.all_to_all(packed, "mesh", split_axis=2, concat_axis=2, tiled=True)
        extended = jnp.concatenate([term, arrived.reshape(2, rows, parts * capacity)], axis=2)
        stencil = jnp.zeros_like(term)
        for apply_order in range(NBRS):
            stencil = stencil + weights[apply_order] * (
                jnp.take(extended, neighbours[apply_order], axis=2) - term
            )
        blocks = jnp.stack(
            [
                jnp.stack([intersection[0], -intersection[1]]),
                jnp.stack([intersection[1], intersection[0]]),
            ]
        )
        exchange = jnp.einsum("dmp,cdmj->cjp", full_frozen, blocks, precision=lax.Precision.HIGHEST)
        image = -0.5 * stencil + potential * term - exchange
        term = time_step / order * rotate(image)
        total = total + term
    return total


def solution(mesh):
    return jax.shard_map(
        body,
        mesh=mesh,
        in_specs=(
            P(None, "band", "mesh"),
            P(None, "band", "mesh"),
            P(None, "mesh"),
            P("mesh"),
            P("mesh", None, None),
            P(None, "mesh"),
        ),
        out_specs=P(None, "band", "mesh"),
        check_vma=False,
    )
```

profile of v0, /device:TPU:0, one launch (start us, length us, event | category | flops | bytes accessed | tf_op | source)
XLA Modules:
  0.0 581.9 jit_solution(13586005560089532101)
XLA Ops:
  2.1 14.4 %gather_fusion = f32[2048,2,16]{2,1,0:T(2,128)} fusion(f32[2,16,1024]{1,0,2:T(2,128)S(1)} %copy.119, s32[2048]{0:T(1024)S(1)} %fusion.108), kind=kCustom, calls=%fused_computation.clone | custom fusion | bytes 532480 | tf_op jit(solution)/shard_map/jit(_take)/gather | solution.py:29
  16.5 10.0 %broadcast_select_fusion.3 = f32[2048,2,16]{2,1,0:T(2,128)S(1)} fusion(f32[2048,2,16]{2,1,0:T(2,128)} %gather_fusion, pred[2048]{0:T(1024)(128)(4,1)S(1)} %compare_and_fusion), kind=kLoop, calls=%fused_computation.39 | loop fusion | flops 65536 | bytes 526336 | tf_op jit(solution)/shard_map/jit(_take)/select_n | solution.py:29
  28.5 5.2 all-to-all-start
  39.6 14.2 %all_gather.3 = f32[2,32,1024]{2,1,0:T(8,128)S(1)} all-gather(f32[2,8,1024]{2,1,0:T(8,128)S(1)} %copy-done.34), channel_id=1, replica_groups=mesh['mesh'=8,'band'=4] {'band'}, dimensions={1}, use_global_device_ids=true | all-gather | bytes 327680 | tf_op jit(solution)/shard_map/all_gather | solution.py:20
  54.3 23.0 %psum.28 = f32[2,32,16]{1,2,0:T(8,128)S(1)} all-reduce(f32[2,32,16]{1,2,0:T(8,128)S(1)} %convolution_bitcast_fusion.7), channel_id=1, replica_groups=mesh['mesh'=8,'band'=4] {'mesh'}, use_global_device_ids=true, to_apply=%region_0.3 | all-reduce | flops 1024 | bytes 8192 | tf_op jit(solution)/shard_map/psum | solution.py:28
  79.9 4.1 copy.122
  84.0 7.6 %gather_fusion.1 = f32[1024,2,16]{2,1,0:T(2,128)} fusion(f32[2,16,3072]{1,0,2:T(2,128)S(1)} %copy.122, s32[1024]{0:T(1024)} %fusion.109), kind=kCustom, calls=%fused_computation.1.clone | custom fusion | bytes 266240 | tf_op jit(solution)/shard_map/jit(_take)/gather | solution.py:35
  93.7 7.6 %gather_fusion.2 = f32[1024,2,16]{2,1,0:T(2,128)} fusion(f32[2,16,3072]{1,0,2:T(2,128)S(1)} %copy.122, s32[1024]{0:T(1024)} %fusion.110), kind=kCustom, calls=%fused_computation.5.clone | custom fusion | bytes 266240 | tf_op jit(solution)/shard_map/jit(_take)/gather | solution.py:35
  103.3 7.6 %gather_fusion.3 = f32[1024,2,16]{2,1,0:T(2,128)} fusion(f32[2,16,3072]{1,0,2:T(2,128)S(1)} %copy.122, s32[1024]{0:T(1024)} %fusion.111), kind=kCustom, calls=%fused_computation.6.clone | custom fusion | bytes 266240 | tf_op jit(solution)/shard_map/jit(_take)/gather | solution.py:35
  110.9 2.0 copy.127
  112.9 7.6 %gather_fusion.4 = f32[1024,2,16]{2,1,0:T(2,128)} fusion(f32[2,16,3072]{1,0,2:T(2,128)S(1)} %copy.122, s32[1024]{0:T(1024)} %fusion.112), kind=kCustom, calls=%fused_computation.7.clone | custom fusion | bytes 266240 | tf_op jit(solution)/shard_map/jit(_take)/gather | solution.py:35
  122.5 7.6 %gather_fusion.5 = f32[1024,2,16]{2,1,0:T(2,128)} fusion(f32[2,16,3072]{1,0,2:T(2,128)S(1)} %copy.122, s32[1024]{0:T(1024)} %fusion.113), kind=kCustom, calls=%fused_computation.8.clone | custom fusion | bytes 266240 | tf_op jit(solution)/shard_map/jit(_take)/gather | solution.py:35
  132.1 7.6 %gather_fusion.6 = f32[1024,2,16]{2,1,0:T(2,128)} fusion(f32[2,16,3072]{1,0,2:T(2,128)S(1)} %copy.122, s32[1024]{0:T(1024)} %fusion.114), kind=kCustom, calls=%fused_computation.9.clone | custom fusion | bytes 266240 | tf_op jit(solution)/shard_map/jit(_take)/gather | solution.py:35
  141.7 7.5 %gather_fusion.7 = f32[1024,2,16]{2,1,0:T(2,128)} fusion(f32[2,16,3072]{1,0,2:T(2,128)S(1)} %copy.122, s32[1024]{0:T(1024)S(1)} %fusion.115), kind=kCustom, calls=%fused_computation.10.clone | custom fusion | bytes 266240 | tf_op jit(solution)/shard_map/jit(_take)/gather | solution.py:35
  151.2 7.5 %gather_fusion.8 = f32[1024,2,16]{2,1,0:T(2,128)} fusion(f32[2,16,3072]{1,0,2:T(2,128)S(1)} %copy.122, s32[1024]{0:T(1024)S(1)} %fusion.116), kind=kCustom, calls=%fused_computation.11.clone | custom fusion | bytes 266240 | tf_op jit(solution)/shard_map/jit(_take)/gather | solution.py:35
  163.5 22.3 %psum.29 = f32[2,32,16]{1,2,0:T(8,128)S(1)} all-reduce(f32[2,32,16]{1,2,0:T(8,128)S(1)} %convolution_bitcast_fusion.6), channel_id=1, replica_groups=mesh['mesh'=8,'band'=4] {'mesh'}, use_global_device_ids=true, to_apply=%region_1.4 | all-reduce | flops 1024 | bytes 8192 | tf_op jit(solution)/shard_map/psum | solution.py:28
  185.8 14.4 %gather_fusion.9 = f32[2048,2,16]{2,1,0:T(2,128)} fusion(f32[2,16,1024]{1,0,2:T(2,128)S(1)} %copy.138, s32[2048]{0:T(1024)S(1)} %fusion.108), kind=kCustom, calls=%fused_computation.2.clone | custom fusion | bytes 532480 | tf_op jit(solution)/shard_map/jit(_take)/gather | solution.py:29
  200.2 10.0 %broadcast_select_fusion.2 = f32[2048,2,16]{2,1,0:T(2,128)S(1)} fusion(f32[2048,2,16]{2,1,0:T(2,128)} %gather_fusion.9, pred[2048]{0:T(1024)(128)(4,1)S(1)} %copy-done.36), kind=kLoop, calls=%fused_computation.38 | loop fusion | flops 65536 | bytes 526336 | tf_op jit(solution)/shard_map/jit(_take)/select_n | solution.py:29
  212.1 3.6 all-to-all-start.1
  216.3 6.1 %all-to-all-done.1 = f32[2,16,8,256]{3,1,0,2:T(8,128)S(1)} async-done(((f32[2,16,8,256]{3,1,0,2:T(8,128)}), f32[2,16,8,256]{3,1,0,2:T(8,128)S(1)}, u32[]{:S(2)}, u32[]{:S(2)}) %all-to-all-start.1) | async-done | bytes 262176 | tf_op jit(solution)/shard_map/all_to_all | solution.py:30
  223.2 4.1 copy.141
  227.3 7.6 %gather_fusion.10 = f32[1024,2,16]{2,1,0:T(2,128)} fusion(f32[2,16,3072]{1,0,2:T(2,128)S(1)} %copy.141, s32[1024]{0:T(1024)} %fusion.109), kind=kCustom, calls=%fused_computation.12.clone | custom fusion | bytes 266240 | tf_op jit(solution)/shard_map/jit(_take)/gather | solution.py:35
  235.0 7.6 %gather_fusion.11 = f32[1024,2,16]{2,1,0:T(2,128)} fusion(f32[2,16,3072]{1,0,2:T(2,128)S(1)} %copy.141, s32[1024]{0:T(1024)} %fusion.110), kind=kCustom, calls=%fused_computation.13.clone | custom fusion | bytes 266240 | tf_op jit(solution)/shard_map/jit(_take)/gather | solution.py:35
  242.6 7.6 %gather_fusion.12 = f32[1024,2,16]{2,1,0:T(2,128)} fusion(f32[2,16,3072]{1,0,2:T(2,128)S(1)} %copy.141, s32[1024]{0:T(1024)} %fusion.111), kind=kCustom, calls=%fused_computation.14.clone | custom fusion | bytes 266240 | tf_op jit(solution)/shard_map/jit(_take)/gather | solution.py:35
  250.2 7.6 %gather_fusion.13 = f32[1024,2,16]{2,1,0:T(2,128)} fusion(f32[2,16,3072]{1,0,2:T(2,128)S(1)} %copy.141, s32[1024]{0:T(1024)} %fusion.112), kind=kCustom, calls=%fused_computation.15.clone | custom fusion | bytes 266240 | tf_op jit(solution)/shard_map/jit(_take)/gather | solution.py:35
  257.8 7.6 %gather_fusion.14 = f32[1024,2,16]{2,1,0:T(2,128)} fusion(f32[2,16,3072]{1,0,2:T(2,128)S(1)} %copy.141, s32[1024]{0:T(1024)} %fusion.113), kind=kCustom, calls=%fused_computation.16.clone | custom fusion | bytes 266240 | tf_op jit(solution)/shard_map/jit(_take)/gather | solution.py:35
  265.4 7.6 %gather_fusion.15 = f32[1024,2,16]{2,1,0:T(2,128)} fusion(f32[2,16,3072]{1,0,2:T(2,128)S(1)} %copy.141, s32[1024]{0:T(1024)} %fusion.114), kind=kCustom, calls=%fused_computation.17.clone | custom fusion | bytes 266240 | tf_op jit(solution)/shard_map/jit(_take)/gather | solution.py:35
  273.0 7.5 %gather_fusion.16 = f32[1024,2,16]{2,1,0:T(2,128)} fusion(f32[2,16,3072]{1,0,2:T(2,128)S(1)} %copy.141, s32[1024]{0:T(1024)S(1)} %fusion.115), kind=kCustom, calls=%fused_computation.18.clone | custom fusion | bytes 266240 | tf_op jit(solution)/shard_map/jit(_take)/gather | solution.py:35
  280.5 7.5 %gather_fusion.17 = f32[1024,2,16]{2,1,0:T(2,128)} fusion(f32[2,16,3072]{1,0,2:T(2,128)S(1)} %copy.141, s32[1024]{0:T(1024)S(1)} %fusion.116), kind=kCustom, calls=%fused_computation.19.clone | custom fusion | bytes 266240 | tf_op jit(solution)/shard_map/jit(_take)/gather | solution.py:35
  288.0 2.1 copy.142
  290.1 2.1 copy.144
  292.2 2.1 copy.146
  303.7 22.3 %psum.30 = f32[2,32,16]{1,2,0:T(8,128)S(1)} all-reduce(f32[2,32,16]{1,2,0:T(8,128)S(1)} %convolution_bitcast_fusion.5), channel_id=1, replica_groups=mesh['mesh'=8,'band'=4] {'mesh'}, use_global_device_ids=true, to_apply=%region_2.5 | all-reduce | flops 1024 | bytes 8192 | tf_op jit(solution)/shard_map/psum | solution.py:28
  326.0 14.4 %gather_fusion.18 = f32[2048,2,16]{2,1,0:T(2,128)} fusion(f32[2,16,1024]{1,0,2:T(2,128)S(1)} %copy.157, s32[2048]{0:T(1024)S(1)} %fusion.108), kind=kCustom, calls=%fused_computation.3.clone | custom fusion | bytes 532480 | tf_op jit(solution)/shard_map/jit(_take)/gather | solution.py:29
  340.4 10.0 %broadcast_select_fusion.1 = f32[2048,2,16]{2,1,0:T(2,128)S(1)} fusion(f32[2048,2,16]{2,1,0:T(2,128)} %gather_fusion.18, pred[2048]{0:T(1024)(128)(4,1)S(1)} %copy-done.37), kind=kLoop, calls=%fused_computation.37 | loop fusion | flops 65536 | bytes 526336 | tf_op jit(solution)/shard_map/jit(_take)/select_n | solution.py:29
  352.3 3.4 all-to-all-start.2
  356.3 6.2 %all-to-all-done.2 = f32[2,16,8,256]{3,1,0,2:T(8,128)S(1)} async-done(((f32[2,16,8,256]{3,1,0,2:T(8,128)}), f32[2,16,8,256]{3,1,0,2:T(8,128)S(1)}, u32[]{:S(2)}, u32[]{:S(2)}) %all-to-all-start.2) | async-done | bytes 262176 | tf_op jit(solution)/shard_map/all_to_all | solution.py:30
  363.4 4.1 copy.160
  367.5 7.6 %gather_fusion.19 = f32[1024,2,16]{2,1,0:T(2,128)} fusion(f32[2,16,3072]{1,0,2:T(2,128)S(1)} %copy.160, s32[1024]{0:T(1024)} %fusion.109), kind=kCustom, calls=%fused_computation.20.clone | custom fusion | bytes 266240 | tf_op jit(solution)/shard_map/jit(_take)/gather | solution.py:35
  375.2 7.6 %gather_fusion.20 = f32[1024,2,16]{2,1,0:T(2,128)} fusion(f32[2,16,3072]{1,0,2:T(2,128)S(1)} %copy.160, s32[1024]{0:T(1024)} %fusion.110), kind=kCustom, calls=%fused_computation.21.clone | custom fusion | bytes 266240 | tf_op jit(solution)/shard_map/jit(_take)/gather | solution.py:35
  382.8 7.6 %gather_fusion.21 = f32[1024,2,16]{2,1,0:T(2,128)} fusion(f32[2,16,3072]{1,0,2:T(2,128)S(1)} %copy.160, s32[1024]{0:T(1024)} %fusion.111), kind=kCustom, calls=%fused_computation.22.clone | custom fusion | bytes 266240 | tf_op jit(solution)/shard_map/jit(_take)/gather | solution.py:35
  390.4 7.6 %gather_fusion.22 = f32[1024,2,16]{2,1,0:T(2,128)} fusion(f32[2,16,3072]{1,0,2:T(2,128)S(1)} %copy.160, s32[1024]{0:T(1024)} %fusion.112), kind=kCustom, calls=%fused_computation.23.clone | custom fusion | bytes 266240 | tf_op jit(solution)/shard_map/jit(_take)/gather | solution.py:35
  398.0 7.6 %gather_fusion.23 = f32[1024,2,16]{2,1,0:T(2,128)} fusion(f32[2,16,3072]{1,0,2:T(2,128)S(1)} %copy.160, s32[1024]{0:T(1024)} %fusion.113), kind=kCustom, calls=%fused_computation.24.clone | custom fusion | bytes 266240 | tf_op jit(solution)/shard_map/jit(_take)/gather | solution.py:35
  405.6 7.6 %gather_fusion.24 = f32[1024,2,16]{2,1,0:T(2,128)} fusion(f32[2,16,3072]{1,0,2:T(2,128)S(1)} %copy.160, s32[1024]{0:T(1024)} %fusion.114), kind=kCustom, calls=%fused_computation.25.clone | custom fusion | bytes 266240 | tf_op jit(solution)/shard_map/jit(_take)/gather | solution.py:35
  413.2 7.5 %gather_fusion.25 = f32[1024,2,16]{2,1,0:T(2,128)} fusion(f32[2,16,3072]{1,0,2:T(2,128)S(1)} %copy.160, s32[1024]{0:T(1024)S(1)} %fusion.115), kind=kCustom, calls=%fused_computation.26.clone | custom fusion | bytes 266240 | tf_op jit(solution)/shard_map/jit(_take)/gather | solution.py:35
  420.7 7.5 %gather_fusion.26 = f32[1024,2,16]{2,1,0:T(2,128)} fusion(f32[2,16,3072]{1,0,2:T(2,128)S(1)} %copy.160, s32[1024]{0:T(1024)S(1)} %fusion.116), kind=kCustom, calls=%fused_computation.27.clone | custom fusion | bytes 266240 | tf_op jit(solution)/shard_map/jit(_take)/gather | solution.py:35
  428.1 2.1 copy.161
  430.2 2.1 copy.163
  432.4 2.1 copy.165
  443.8 22.3 %psum.31 = f32[2,32,16]{1,2,0:T(8,128)S(1)} all-reduce(f32[2,32,16]{1,2,0:T(8,128)S(1)} %convolution_bitcast_fusion.4), channel_id=1, replica_groups=mesh['mesh'=8,'band'=4] {'mesh'}, use_global_device_ids=true, to_apply=%region_3.6 | all-reduce | flops 1024 | bytes 8192 | tf_op jit(solution)/shard_map/psum | solution.py:28
  466.1 14.4 %gather_fusion.27 = f32[2048,2,16]{2,1,0:T(2,128)} fusion(f32[2,16,1024]{1,0,2:T(2,128)S(1)} %copy.176, s32[2048]{0:T(1024)S(1)} %fusion.108), kind=kCustom, calls=%fused_computation.4.clone | custom fusion | bytes 532480 | tf_op jit(solution)/shard_map/jit(_take)/gather | solution.py:29
  480.6 10.0 %broadcast_select_fusion = f32[2048,2,16]{2,1,0:T(2,128)S(1)} fusion(f32[2048,2,16]{2,1,0:T(2,128)} %gather_fusion.27, pred[2048]{0:T(1024)(128)(4,1)S(1)} %copy-done.38), kind=kLoop, calls=%fused_computation.36 | loop fusion | flops 65536 | bytes 526336 | tf_op jit(solution)/shard_map/jit(_take)/select_n | solution.py:29
  492.4 3.8 all-to-all-start.3
  496.8 6.0 %all-to-all-done.3 = f32[2,16,8,256]{3,1,0,2:T(8,128)S(1)} async-done(((f32[2,16,8,256]{3,1,0,2:T(8,128)}), f32[2,16,8,256]{3,1,0,2:T(8,128)S(1)}, u32[]{:S(2)}, u32[]{:S(2)}) %all-to-all-start.3) | async-done | bytes 262176 | tf_op jit(solution)/shard_map/all_to_all | solution.py:30
  503.7 4.1 copy.179
  507.8 7.6 %gather_fusion.28 = f32[1024,2,16]{2,1,0:T(2,128)} fusion(f32[2,16,3072]{1,0,2:T(2,128)S(1)} %copy.179, s32[1024]{0:T(1024)} %fusion.109), kind=kCustom, calls=%fused_computation.28.clone | custom fusion | bytes 266240 | tf_op jit(solution)/shard_map/jit(_take)/gather | solution.py:35
  515.4 7.6 %gather_fusion.29 = f32[1024,2,16]{2,1,0:T(2,128)} fusion(f32[2,16,3072]{1,0,2:T(2,128)S(1)} %copy.179, s32[1024]{0:T(1024)} %fusion.110), kind=kCustom, calls=%fused_computation.29.clone | custom fusion | bytes 266240 | tf_op jit(solution)/shard_map/jit(_take)/gather | solution.py:35
  523.0 7.6 %gather_fusion.30 = f32[1024,2,16]{2,1,0:T(2,128)} fusion(f32[2,16,3072]{1,0,2:T(2,128)S(1)} %copy.179, s32[1024]{0:T(1024)} %fusion.111), kind=kCustom, calls=%fused_computation.30.clone | custom fusion | bytes 266240 | tf_op jit(solution)/shard_map/jit(_take)/gather | solution.py:35
  530.6 7.6 %gather_fusion.31 = f32[1024,2,16]{2,1,0:T(2,128)} fusion(f32[2,16,3072]{1,0,2:T(2,128)S(1)} %copy.179, s32[1024]{0:T(1024)} %fusion.112), kind=kCustom, calls=%fused_computation.31.clone | custom fusion | bytes 266240 | tf_op jit(solution)/shard_map/jit(_take)/gather | solution.py:35
  538.2 7.5 %gather_fusion.32 = f32[1024,2,16]{2,1,0:T(2,128)} fusion(f32[2,16,3072]{1,0,2:T(2,128)S(1)} %copy.179, s32[1024]{0:T(1024)S(1)} %copy-done.29), kind=kCustom, calls=%fused_computation.32.clone | custom fusion | bytes 266240 | tf_op jit(solution)/shard_map/jit(_take)/gather | solution.py:35
  545.7 7.5 %gather_fusion.33 = f32[1024,2,16]{2,1,0:T(2,128)} fusion(f32[2,16,3072]{1,0,2:T(2,128)S(1)} %copy.179, s32[1024]{0:T(1024)S(1)} %copy-done.28), kind=kCustom, calls=%fused_computation.33.clone | custom fusion | bytes 266240 | tf_op jit(solution)/shard_map/jit(_take)/gather | solution.py:35
  553.2 7.5 %gather_fusion.34 = f32[1024,2,16]{2,1,0:T(2,128)} fusion(f32[2,16,3072]{1,0,2:T(2,128)S(1)} %copy.179, s32[1024]{0:T(1024)S(1)} %fusion.115), kind=kCustom, calls=%fused_computation.34.clone | custom fusion | bytes 266240 | tf_op jit(solution)/shard_map/jit(_take)/gather | solution.py:35
  560.7 7.5 %gather_fusion.35 = f32[1024,2,16]{2,1,0:T(2,128)} fusion(f32[2,16,3072]{1,0,2:T(2,128)S(1)} %copy.179, s32[1024]{0:T(1024)S(1)} %fusion.116), kind=kCustom, calls=%fused_computation.35.clone | custom fusion | bytes 266240 | tf_op jit(solution)/shard_map/jit(_take)/gather | solution.py:35
  568.2 2.2 copy.180
  (178 shorter events, 69.4 us)
Async XLA Ops:
  0.7 27.7 %copy-start.35 = (pred[2048]{0:T(1024)(128)(4,1)}, pred[2048]{0:T(1024)(128)(4,1)S(1)}, u32[]{:S(2)}) copy-start(pred[2048]{0:T(1024)(128)(4,1)S(1)} %compare_and_fusion) | copy-start | bytes 6148
  16.5 17.1 %copy-start = (f32[2,16,1024]{2,1,0:T(8,128)S(1)}, f32[2,16,1024]{2,1,0:T(8,128)}, u32[]{:S(2)}) copy-start(f32[2,16,1024]{2,1,0:T(8,128)} %param.10) | copy-start | bytes 393220
  16.5 17.1 %copy-start.39 = (s32[8,1024]{1,0:T(8,128)S(1)}, s32[8,1024]{1,0:T(8,128)}, u32[]{:S(2)}) copy-start(s32[8,1024]{1,0:T(8,128)} %param.15) | copy-start | bytes 98308
  16.5 23.1 %copy-start.34 = (f32[2,8,1024]{2,1,0:T(8,128)S(1)}, f32[2,8,1024]{2,1,0:T(8,128)}, u32[]{:S(2)}) copy-start(f32[2,8,1024]{2,1,0:T(8,128)} %param.11) | copy-start | bytes 196612
  26.5 50.7 %copy-start.41 = (f32[1024]{0:T(1024)S(1)}, f32[1024]{0:T(1024)}, u32[]{:S(2)}) copy-start(f32[1024]{0:T(1024)} %param.13) | copy-start | bytes 12292
  26.6 51.9 %copy-start.40 = (f32[8,1024]{1,0:T(8,128)S(1)}, f32[8,1024]{1,0:T(8,128)}, u32[]{:S(2)}) copy-start(f32[8,1024]{1,0:T(8,128)} %param.12) | copy-start | bytes 98308
  28.5 50.6 %all-to-all-start = ((f32[2,16,8,256]{3,1,0,2:T(8,128)}), f32[2,16,8,256]{3,1,0,2:T(8,128)S(1)}, u32[]{:S(2)}, u32[]{:S(2)}) async-start(f32[2,16,8,256]{3,1,0,2:T(8,128)} %copy.120), calls=%async_computation | async-start | bytes 524288 | tf_op jit(solution)/shard_map/all_to_all | solution.py:30
  158.7 41.6 %copy-start.36 = (pred[2048]{0:T(1024)(128)(4,1)S(1)}, pred[2048]{0:T(1024)(128)(4,1)}, u32[]{:S(2)}) copy-start(pred[2048]{0:T(1024)(128)(4,1)} %copy-done.35) | copy-start | bytes 6148
  161.9 0.6 copy-start.11
  161.9 0.6 copy-start.13
  212.1 10.3 %all-to-all-start.1 = ((f32[2,16,8,256]{3,1,0,2:T(8,128)}), f32[2,16,8,256]{3,1,0,2:T(8,128)S(1)}, u32[]{:S(2)}, u32[]{:S(2)}) async-start(f32[2,16,8,256]{3,1,0,2:T(8,128)} %copy.139), calls=%async_computation.1 | async-start | bytes 524288 | tf_op jit(solution)/shard_map/all_to_all | solution.py:30
  287.9 10.4 %copy-start.9 = (f32[1024,2,16]{2,1,0:T(2,128)S(1)}, f32[1024,2,16]{2,1,0:T(2,128)}, u32[]{:S(2)}) copy-start(f32[1024,2,16]{2,1,0:T(2,128)} %gather_fusion.15) | copy-start | bytes 393220
  290.0 9.3 %copy-start.7 = (f32[1024,2,16]{2,1,0:T(2,128)S(1)}, f32[1024,2,16]{2,1,0:T(2,128)}, u32[]{:S(2)}) copy-start(f32[1024,2,16]{2,1,0:T(2,128)} %gather_fusion.16) | copy-start | bytes 393220
  292.2 7.6 %copy-start.5 = (f32[1024,2,16]{2,1,0:T(2,128)S(1)}, f32[1024,2,16]{2,1,0:T(2,128)}, u32[]{:S(2)}) copy-start(f32[1024,2,16]{2,1,0:T(2,128)} %gather_fusion.17) | copy-start | bytes 393220
  299.8 40.6 %copy-start.37 = (pred[2048]{0:T(1024)(128)(4,1)S(1)}, pred[2048]{0:T(1024)(128)(4,1)}, u32[]{:S(2)}) copy-start(pred[2048]{0:T(1024)(128)(4,1)} %copy-done.35) | copy-start | bytes 6148
  302.1 0.6 copy-start.15
  302.1 0.6 copy-start.17
  352.3 10.3 %all-to-all-start.2 = ((f32[2,16,8,256]{3,1,0,2:T(8,128)}), f32[2,16,8,256]{3,1,0,2:T(8,128)S(1)}, u32[]{:S(2)}, u32[]{:S(2)}) async-start(f32[2,16,8,256]{3,1,0,2:T(8,128)} %copy.158), calls=%async_computation.2 | async-start | bytes 524288 | tf_op jit(solution)/shard_map/all_to_all | solution.py:30
  428.1 10.4 %copy-start.10 = (f32[1024,2,16]{2,1,0:T(2,128)S(1)}, f32[1024,2,16]{2,1,0:T(2,128)}, u32[]{:S(2)}) copy-start(f32[1024,2,16]{2,1,0:T(2,128)} %gather_fusion.24) | copy-start | bytes 393220
  430.2 9.3 %copy-start.8 = (f32[1024,2,16]{2,1,0:T(2,128)S(1)}, f32[1024,2,16]{2,1,0:T(2,128)}, u32[]{:S(2)}) copy-start(f32[1024,2,16]{2,1,0:T(2,128)} %gather_fusion.25) | copy-start | bytes 393220
  432.4 7.6 %copy-start.6 = (f32[1024,2,16]{2,1,0:T(2,128)S(1)}, f32[1024,2,16]{2,1,0:T(2,128)}, u32[]{:S(2)}) copy-start(f32[1024,2,16]{2,1,0:T(2,128)} %gather_fusion.26) | copy-start | bytes 393220
  440.0 40.6 %copy-start.38 = (pred[2048]{0:T(1024)(128)(4,1)S(1)}, pred[2048]{0:T(1024)(128)(4,1)}, u32[]{:S(2)}) copy-start(pred[2048]{0:T(1024)(128)(4,1)} %copy-done.35) | copy-start | bytes 6148
  442.2 0.6 copy-start.19
  442.2 0.6 copy-start.21
  492.4 45.7 %copy-start.29 = (s32[1024]{0:T(1024)S(1)}, s32[1024]{0:T(1024)}, u32[]{:S(2)}) copy-start(s32[1024]{0:T(1024)} %fusion.113) | copy-start | bytes 12292
  492.4 10.4 %all-to-all-start.3 = ((f32[2,16,8,256]{3,1,0,2:T(8,128)}), f32[2,16,8,256]{3,1,0,2:T(8,128)S(1)}, u32[]{:S(2)}, u32[]{:S(2)}) async-start(f32[2,16,8,256]{3,1,0,2:T(8,128)} %copy.177), calls=%async_computation.3 | async-start | bytes 524288 | tf_op jit(solution)/shard_map/all_to_all | solution.py:30
  496.2 49.5 %copy-start.28 = (s32[1024]{0:T(1024)S(1)}, s32[1024]{0:T(1024)}, u32[]{:S(2)}) copy-start(s32[1024]{0:T(1024)} %fusion.114) | copy-start | bytes 12292
  568.2 6.2 %copy-start.1 = (f32[1024,2,16]{2,1,0:T(2,128)S(1)}, f32[1024,2,16]{2,1,0:T(2,128)}, u32[]{:S(2)}) copy-start(f32[1024,2,16]{2,1,0:T(2,128)} %gather_fusion.31) | copy-start | bytes 393220
  568.2 7.3 %copy-start.2 = (f32[1024,2,16]{2,1,0:T(2,128)S(1)}, f32[1024,2,16]{2,1,0:T(2,128)}, u32[]{:S(2)}) copy-start(f32[1024,2,16]{2,1,0:T(2,128)} %gather_fusion.32) | copy-start | bytes 393220
  568.2 8.4 %copy-start.3 = (f32[1024,2,16]{2,1,0:T(2,128)S(1)}, f32[1024,2,16]{2,1,0:T(2,128)}, u32[]{:S(2)}) copy-start(f32[1024,2,16]{2,1,0:T(2,128)} %gather_fusion.33) | copy-start | bytes 393220
  574.4 5.2 copy-start.30
  574.4 5.2 copy-start.31
  574.4 5.2 copy-start.32
  574.4 5.2 copy-start.33
  575.5 3.6 copy-start.4
  576.6 3.0 copy-start.20
  576.6 3.0 copy-start.22
  576.6 3.0 copy-start.23
  576.6 3.0 copy-start.24
  576.6 3.0 copy-start.25
  576.6 3.0 copy-start.26
  576.6 3.0 copy-start.27
  576.6 4.5 copy-start.12
  576.7 4.5 copy-start.14
  576.7 4.5 copy-start.16
  576.7 4.5 copy-start.18
where the time goes:
time: 585 us; the launch traced here: 582 us
  local copies, waits for them, and re-layouts  382 us (65%)
  blocking collectives  104 us (18%)
  other arithmetic  53 us (9%)
  waiting for transfers between devices  18.3 us (3%)
  starting transfers between devices  15.9 us (3%)
  matrix products  8.07 us (1%)
    gather x64, local copies, waits for them, and re-layouts, body(): jnp.take(extended, neighbours[apply_order], axis=2) - term  293 us
    psum x4, blocking collectives, body(): intersection = lax.psum(partial_intersection, 'mesh')  89.9 us
    gather x4, local copies, waits for them, and re-layouts, body(): jnp.take(term, routes.reshape(-1), axis=2).reshape(2, rows, parts, capacity)  57.7 us
    select_n x4, other arithmetic, body(): jnp.take(term, routes.reshape(-1), axis=2).reshape(2, rows, parts, capacity)  39.9 us
    all_to_all x4, waiting for transfers between devices, body(): lax.all_to_all(packed, 'mesh', split_axis=2, concat_axis=2, tiled=True)  18.3 us
    concatenate x4, local copies, waits for them, and re-layouts, body(): jnp.concatenate([term, arrived.reshape(2, rows, parts * capacity)], axis=2)  16.6 us
    all_to_all x4, starting transfers between devices, body(): lax.all_to_all(packed, 'mesh', split_axis=2, concat_axis=2, tiled=True)  15.9 us
    all_gather x1, blocking collectives, body(): full_frozen = lax.all_gather(frozen, 'band', axis=1, tiled=True)  14.2 us
  transfers between devices with their start and end apart: 4, of which 3 were waited for; matrix products, arithmetic and copies ran while one was open for 2% of the time, Pallas kernels for 0%

commit v1 on v0

--- a/solution.py
+++ b/solution.py
@@ -17,7 +17,12 @@
     rows = states.shape[1]
     capacity = send_list.shape[2]
     routes = send_list[0]
-    full_frozen = lax.all_gather(frozen, "band", axis=1, tiled=True)
+    ring = [frozen]
+    for hop in range(3):
+        ring.append(lax.ppermute(ring[-1], "band", [(dev, (dev + 1) % 4) for dev in range(4)]))
+    full_frozen = jnp.roll(
+        jnp.concatenate(ring[::-1], axis=1), (lax.axis_index("band") + 1) * ring[0].shape[1], axis=1
+    )
     total = states
     term = states
     for order in range(1, TERMS + 1):

time: 585 us -> 552 us (0.944)
  local copies, waits for them, and re-layouts: 382 us -> 361 us
  blocking collectives: 104 us -> 89.3 us
  waiting for transfers between devices: 18.3 us -> 29 us
  other arithmetic: 53 us -> 43.5 us
    gather x64, local copies, waits for them, and re-layouts: 293 us -> 278 us  [body(): jnp.take(extended, neighbours[apply_order], axis=2) - term]
    all_gather x1 -> x0, blocking collectives: 14.2 us -> none  [body(): full_frozen = lax.all_gather(frozen, 'band', axis=1, tiled=True)]
    ppermute x0 -> x3, waiting for transfers between devices: none -> 10.7 us  [body(): lax.ppermute(ring[-1], 'band', [(dev, (dev + 1) % 4) for dev in range(4)])]
  transfers between devices with their start and end apart: 4 -> 7, of which waited for: 3 -> 5; matrix products, arithmetic and copies ran while one was open for 2% -> 6% of each run, Pallas kernels for 0% -> 0%
where the time goes in v1:
time: 552 us; the launch traced here: 549 us
  local copies, waits for them, and re-layouts  361 us (65%)
  blocking collectives  89.3 us (16%)
  other arithmetic  43.5 us (8%)
  waiting for transfers between devices  29 us (5%)
  starting transfers between devices  19 us (3%)
    gather x64, local copies, waits for them, and re-layouts, body(): jnp.take(extended, neighbours[apply_order], axis=2) - term  278 us
    psum x4, blocking collectives, body(): intersection = lax.psum(partial_intersection, 'mesh')  89.3 us
    gather x4, local copies, waits for them, and re-layouts, body(): jnp.take(term, routes.reshape(-1), axis=2).reshape(2, rows, parts, capacity)  57.7 us
    select_n x4, other arithmetic, body(): jnp.take(term, routes.reshape(-1), axis=2).reshape(2, rows, parts, capacity)  39.9 us
    all_to_all x4, waiting for transfers between devices, body(): lax.all_to_all(packed, 'mesh', split_axis=2, concat_axis=2, tiled=True)  18.3 us
    all_to_all x4, starting transfers between devices, body(): lax.all_to_all(packed, 'mesh', split_axis=2, concat_axis=2, tiled=True)  14.4 us
    concatenate x4, local copies, waits for them, and re-layouts, body(): jnp.concatenate([term, arrived.reshape(2, rows, parts * capacity)], axis=2)  13.3 us
  transfers between devices with their start and end apart: 7, of which 5 were waited for; matrix products, arithmetic and copies ran while one was open for 6% of the time, Pallas kernels for 0%

profile of v1, /device:TPU:0, one launch (start us, length us, event | category | flops | bytes accessed | tf_op | source)
XLA Modules:
  0.0 548.6 jit_solution(5495434960226280520)
XLA Ops:
  0.0 3.0 collective-permute-start
  5.1 14.4 %gather_fusion = f32[2048,2,16]{2,1,0:T(2,128)} fusion(f32[2,16,1024]{1,0,2:T(2,128)S(1)} %copy.119, s32[2048]{0:T(1024)S(1)} %fusion.116), kind=kCustom, calls=%fused_computation.clone | custom fusion | bytes 532480 | tf_op jit(solution)/shard_map/jit(_take)/gather | solution.py:34
  19.6 10.0 %broadcast_select_fusion.3 = f32[2048,2,16]{2,1,0:T(2,128)S(1)} fusion(f32[2048,2,16]{2,1,0:T(2,128)} %gather_fusion, pred[2048]{0:T(1024)(128)(4,1)S(1)} %compare_and_fusion), kind=kLoop, calls=%fused_computation.39 | loop fusion | flops 65536 | bytes 526336 | tf_op jit(solution)/shard_map/jit(_take)/select_n | solution.py:34
  31.5 3.7 all-to-all-start
  37.9 4.7 collective-permute-done.1
  42.6 6.0 %collective-permute-done.2 = f32[2,8,1024]{2,1,0:T(8,128)S(1)} collective-permute-done((f32[2,8,1024]{2,1,0:T(8,128)S(1)}, f32[2,8,1024]{2,1,0:T(8,128)S(1)}, u32[]{:S(2)}, u32[]{:S(2)}) %collective-permute-start.2) | collective-permute-done | bytes 65568 | tf_op jit(solution)/shard_map/ppermute | solution.py:22
  49.1 22.4 %psum.28 = f32[2,32,16]{1,2,0:T(8,128)S(1)} all-reduce(f32[2,32,16]{1,2,0:T(8,128)S(1)} %convolution_bitcast_fusion.7), channel_id=1, replica_groups=mesh['mesh'=8,'band'=4] {'mesh'}, use_global_device_ids=true, to_apply=%region_0.3 | all-reduce | flops 1024 | bytes 8192 | tf_op jit(solution)/shard_map/psum | solution.py:33
  71.6 3.3 copy.122
  74.9 5.4 gather_fusion.1
  80.8 5.4 gather_fusion.2
  86.6 5.4 gather_fusion.3
  92.5 5.4 gather_fusion.4
  98.4 5.4 gather_fusion.5
  104.3 5.4 gather_fusion.6
  110.1 5.4 gather_fusion.7
  116.0 5.4 gather_fusion.8
  123.5 22.3 %psum.29 = f32[2,32,16]{1,2,0:T(8,128)S(1)} all-reduce(f32[2,32,16]{1,2,0:T(8,128)S(1)} %convolution_bitcast_fusion.6), channel_id=1, replica_groups=mesh['mesh'=8,'band'=4] {'mesh'}, use_global_device_ids=true, to_apply=%region_1.4 | all-reduce | flops 1024 | bytes 8192 | tf_op jit(solution)/shard_map/psum | solution.py:33
  145.8 14.4 %gather_fusion.9 = f32[2048,2,16]{2,1,0:T(2,128)} fusion(f32[2,16,1024]{1,0,2:T(2,128)S(1)} %copy.138, s32[2048]{0:T(1024)S(1)} %fusion.116), kind=kCustom, calls=%fused_computation.2.clone | custom fusion | bytes 532480 | tf_op jit(solution)/shard_map/jit(_take)/gather | solution.py:34
  160.2 10.0 %broadcast_select_fusion.2 = f32[2048,2,16]{2,1,0:T(2,128)S(1)} fusion(f32[2048,2,16]{2,1,0:T(2,128)} %gather_fusion.9, pred[2048]{0:T(1024)(128)(4,1)S(1)} %compare_and_fusion), kind=kLoop, calls=%fused_computation.38 | loop fusion | flops 65536 | bytes 526336 | tf_op jit(solution)/shard_map/jit(_take)/select_n | solution.py:34
  170.2 1.9 copy.139
  172.1 3.6 all-to-all-start.1
  176.3 6.1 %all-to-all-done.1 = f32[2,16,8,256]{3,1,0,2:T(8,128)S(1)} async-done(((f32[2,16,8,256]{3,1,0,2:T(8,128)}), f32[2,16,8,256]{3,1,0,2:T(8,128)S(1)}, u32[]{:S(2)}, u32[]{:S(2)}) %all-to-all-start.1) | async-done | bytes 262176 | tf_op jit(solution)/shard_map/all_to_all | solution.py:35
  182.4 3.3 copy.141
  185.8 9.4 %gather_fusion.10 = f32[1024,2,16]{2,1,0:T(2,128)} fusion(f32[2,16,3072]{1,0,2:T(2,128)} %copy.141, s32[1024]{0:T(1024)S(1)} %get-tuple-element.68), kind=kCustom, calls=%fused_computation.12.clone | custom fusion | bytes 266240 | tf_op jit(solution)/shard_map/jit(_take)/gather | solution.py:40
  195.1 9.4 %gather_fusion.11 = f32[1024,2,16]{2,1,0:T(2,128)} fusion(f32[2,16,3072]{1,0,2:T(2,128)} %copy.141, s32[1024]{0:T(1024)S(1)} %get-tuple-element.69), kind=kCustom, calls=%fused_computation.13.clone | custom fusion | bytes 266240 | tf_op jit(solution)/shard_map/jit(_take)/gather | solution.py:40
  204.5 9.4 %gather_fusion.12 = f32[1024,2,16]{2,1,0:T(2,128)} fusion(f32[2,16,3072]{1,0,2:T(2,128)} %copy.141, s32[1024]{0:T(1024)S(1)} %get-tuple-element.70), kind=kCustom, calls=%fused_computation.14.clone | custom fusion | bytes 266240 | tf_op jit(solution)/shard_map/jit(_take)/gather | solution.py:40
  213.9 9.4 %gather_fusion.13 = f32[1024,2,16]{2,1,0:T(2,128)} fusion(f32[2,16,3072]{1,0,2:T(2,128)} %copy.141, s32[1024]{0:T(1024)S(1)} %get-tuple-element.71), kind=kCustom, calls=%fused_computation.15.clone | custom fusion | bytes 266240 | tf_op jit(solution)/shard_map/jit(_take)/gather | solution.py:40
  223.3 9.4 %gather_fusion.14 = f32[1024,2,16]{2,1,0:T(2,128)} fusion(f32[2,16,3072]{1,0,2:T(2,128)} %copy.141, s32[1024]{0:T(1024)S(1)} %get-tuple-element.72), kind=kCustom, calls=%fused_computation.16.clone | custom fusion | bytes 266240 | tf_op jit(solution)/shard_map/jit(_take)/gather | solution.py:40
  232.6 9.4 %gather_fusion.15 = f32[1024,2,16]{2,1,0:T(2,128)} fusion(f32[2,16,3072]{1,0,2:T(2,128)} %copy.141, s32[1024]{0:T(1024)S(1)} %get-tuple-element.73), kind=kCustom, calls=%fused_computation.17.clone | custom fusion | bytes 266240 | tf_op jit(solution)/shard_map/jit(_take)/gather | solution.py:40
  242.0 5.4 gather_fusion.16
  247.5 5.4 gather_fusion.17
  259.8 2.0 copy.152
  265.9 22.3 %psum.30 = f32[2,32,16]{1,2,0:T(8,128)S(1)} all-reduce(f32[2,32,16]{1,2,0:T(8,128)S(1)} %convolution_bitcast_fusion.5), channel_id=1, replica_groups=mesh['mesh'=8,'band'=4] {'mesh'}, use_global_device_ids=true, to_apply=%region_2.5 | all-reduce | flops 1024 | bytes 8192 | tf_op jit(solution)/shard_map/psum | solution.py:33
  288.2 14.4 %gather_fusion.18 = f32[2048,2,16]{2,1,0:T(2,128)} fusion(f32[2,16,1024]{1,0,2:T(2,128)S(1)} %copy.157, s32[2048]{0:T(1024)S(1)} %fusion.116), kind=kCustom, calls=%fused_computation.3.clone | custom fusion | bytes 532480 | tf_op jit(solution)/shard_map/jit(_take)/gather | solution.py:34
  302.6 10.0 %broadcast_select_fusion.1 = f32[2048,2,16]{2,1,0:T(2,128)S(1)} fusion(f32[2048,2,16]{2,1,0:T(2,128)} %gather_fusion.18, pred[2048]{0:T(1024)(128)(4,1)S(1)} %copy-done.45), kind=kLoop, calls=%fused_computation.37 | loop fusion | flops 65536 | bytes 526336 | tf_op jit(solution)/shard_map/jit(_take)/select_n | solution.py:34
  312.6 1.9 copy.158
  314.5 3.4 all-to-all-start.2
  318.5 6.2 %all-to-all-done.2 = f32[2,16,8,256]{3,1,0,2:T(8,128)S(1)} async-done(((f32[2,16,8,256]{3,1,0,2:T(8,128)}), f32[2,16,8,256]{3,1,0,2:T(8,128)S(1)}, u32[]{:S(2)}, u32[]{:S(2)}) %all-to-all-start.2) | async-done | bytes 262176 | tf_op jit(solution)/shard_map/all_to_all | solution.py:35
  324.9 3.3 copy.160
  328.2 9.4 %gather_fusion.19 = f32[1024,2,16]{2,1,0:T(2,128)} fusion(f32[2,16,3072]{1,0,2:T(2,128)} %copy.160, s32[1024]{0:T(1024)S(1)} %copy-done.37), kind=kCustom, calls=%fused_computation.20.clone | custom fusion | bytes 266240 | tf_op jit(solution)/shard_map/jit(_take)/gather | solution.py:40
  337.5 9.4 %gather_fusion.20 = f32[1024,2,16]{2,1,0:T(2,128)} fusion(f32[2,16,3072]{1,0,2:T(2,128)} %copy.160, s32[1024]{0:T(1024)S(1)} %copy-done.31), kind=kCustom, calls=%fused_computation.21.clone | custom fusion | bytes 266240 | tf_op jit(solution)/shard_map/jit(_take)/gather | solution.py:40
  346.9 9.4 %gather_fusion.21 = f32[1024,2,16]{2,1,0:T(2,128)} fusion(f32[2,16,3072]{1,0,2:T(2,128)} %copy.160, s32[1024]{0:T(1024)S(1)} %copy-done.40), kind=kCustom, calls=%fused_computation.22.clone | custom fusion | bytes 266240 | tf_op jit(solution)/shard_map/jit(_take)/gather | solution.py:40
  356.3 9.4 %gather_fusion.22 = f32[1024,2,16]{2,1,0:T(2,128)} fusion(f32[2,16,3072]{1,0,2:T(2,128)} %copy.160, s32[1024]{0:T(1024)S(1)} %copy-done.34), kind=kCustom, calls=%fused_computation.23.clone | custom fusion | bytes 266240 | tf_op jit(solution)/shard_map/jit(_take)/gather | solution.py:40
  365.7 9.4 %gather_fusion.23 = f32[1024,2,16]{2,1,0:T(2,128)} fusion(f32[2,16,3072]{1,0,2:T(2,128)} %copy.160, s32[1024]{0:T(1024)S(1)} %copy-done.28), kind=kCustom, calls=%fused_computation.24.clone | custom fusion | bytes 266240 | tf_op jit(solution)/shard_map/jit(_take)/gather | solution.py:40
  375.0 9.4 %gather_fusion.24 = f32[1024,2,16]{2,1,0:T(2,128)} fusion(f32[2,16,3072]{1,0,2:T(2,128)} %copy.160, s32[1024]{0:T(1024)S(1)} %copy-done.25), kind=kCustom, calls=%fused_computation.25.clone | custom fusion | bytes 266240 | tf_op jit(solution)/shard_map/jit(_take)/gather | solution.py:40
  384.4 5.4 gather_fusion.25
  389.9 5.4 gather_fusion.26
  400.9 2.0 copy.169
  402.9 2.0 copy.171
  409.0 22.3 %psum.31 = f32[2,32,16]{1,2,0:T(8,128)S(1)} all-reduce(f32[2,32,16]{1,2,0:T(8,128)S(1)} %convolution_bitcast_fusion.4), channel_id=1, replica_groups=mesh['mesh'=8,'band'=4] {'mesh'}, use_global_device_ids=true, to_apply=%region_3.6 | all-reduce | flops 1024 | bytes 8192 | tf_op jit(solution)/shard_map/psum | solution.py:33
  431.3 14.4 %gather_fusion.27 = f32[2048,2,16]{2,1,0:T(2,128)} fusion(f32[2,16,1024]{1,0,2:T(2,128)S(1)} %copy.176, s32[2048]{0:T(1024)S(1)} %fusion.116), kind=kCustom, calls=%fused_computation.4.clone | custom fusion | bytes 532480 | tf_op jit(solution)/shard_map/jit(_take)/gather | solution.py:34
  445.7 10.0 %broadcast_select_fusion = f32[2048,2,16]{2,1,0:T(2,128)S(1)} fusion(f32[2048,2,16]{2,1,0:T(2,128)} %gather_fusion.27, pred[2048]{0:T(1024)(128)(4,1)S(1)} %copy-done.46), kind=kLoop, calls=%fused_computation.36 | loop fusion | flops 65536 | bytes 526336 | tf_op jit(solution)/shard_map/jit(_take)/select_n | solution.py:34
  457.6 3.6 all-to-all-start.3
  461.9 6.0 %all-to-all-done.3 = f32[2,16,8,256]{3,1,0,2:T(8,128)S(1)} async-done(((f32[2,16,8,256]{3,1,0,2:T(8,128)}), f32[2,16,8,256]{3,1,0,2:T(8,128)S(1)}, u32[]{:S(2)}, u32[]{:S(2)}) %all-to-all-start.3) | async-done | bytes 262176 | tf_op jit(solution)/shard_map/all_to_all | solution.py:35
  468.0 3.3 copy.179
  471.3 5.4 gather_fusion.28
  476.7 5.4 gather_fusion.29
  482.2 9.4 %gather_fusion.30 = f32[1024,2,16]{2,1,0:T(2,128)} fusion(f32[2,16,3072]{1,0,2:T(2,128)} %copy.179, s32[1024]{0:T(1024)S(1)} %copy-done.41), kind=kCustom, calls=%fused_computation.30.clone | custom fusion | bytes 266240 | tf_op jit(solution)/shard_map/jit(_take)/gather | solution.py:40
  491.6 9.4 %gather_fusion.31 = f32[1024,2,16]{2,1,0:T(2,128)} fusion(f32[2,16,3072]{1,0,2:T(2,128)} %copy.179, s32[1024]{0:T(1024)S(1)} %copy-done.35), kind=kCustom, calls=%fused_computation.31.clone | custom fusion | bytes 266240 | tf_op jit(solution)/shard_map/jit(_take)/gather | solution.py:40
  500.9 9.4 %gather_fusion.32 = f32[1024,2,16]{2,1,0:T(2,128)} fusion(f32[2,16,3072]{1,0,2:T(2,128)} %copy.179, s32[1024]{0:T(1024)S(1)} %copy-done.29), kind=kCustom, calls=%fused_computation.32.clone | custom fusion | bytes 266240 | tf_op jit(solution)/shard_map/jit(_take)/gather | solution.py:40
  510.3 9.4 %gather_fusion.33 = f32[1024,2,16]{2,1,0:T(2,128)} fusion(f32[2,16,3072]{1,0,2:T(2,128)} %copy.179, s32[1024]{0:T(1024)S(1)} %copy-done.26), kind=kCustom, calls=%fused_computation.33.clone | custom fusion | bytes 266240 | tf_op jit(solution)/shard_map/jit(_take)/gather | solution.py:40
  519.7 9.4 %gather_fusion.34 = f32[1024,2,16]{2,1,0:T(2,128)} fusion(f32[2,16,3072]{1,0,2:T(2,128)} %copy.179, s32[1024]{0:T(1024)S(1)} %copy-done.23), kind=kCustom, calls=%fused_computation.34.clone | custom fusion | bytes 266240 | tf_op jit(solution)/shard_map/jit(_take)/gather | solution.py:40
  529.1 9.4 %gather_fusion.35 = f32[1024,2,16]{2,1,0:T(2,128)} fusion(f32[2,16,3072]{1,0,2:T(2,128)} %copy.179, s32[1024]{0:T(1024)S(1)} %copy-done.20), kind=kCustom, calls=%fused_computation.35.clone | custom fusion | bytes 266240 | tf_op jit(solution)/shard_map/jit(_take)/gather | solution.py:40
  540.8 2.0 copy.186
  (237 shorter events, 43.7 us)
Async XLA Ops:
  0.0 36.2 %collective-permute-start = (f32[2,8,1024]{2,1,0:T(8,128)}, f32[2,8,1024]{2,1,0:T(8,128)S(1)}, u32[]{:S(2)}, u32[]{:S(2)}) collective-permute-start(f32[2,8,1024]{2,1,0:T(8,128)} %param.11), channel_id=1, source_target_pairs={{0,1},{1,2},{2,3},{3,0},{4,5},{5,6},{6,7},{7,4},{8,9},{9,10},{10,1... | collective-permute-start | bytes 196616 | tf_op jit(solution)/shard_map/ppermute | solution.py:22
  3.7 156.5 %copy-start.44 = (pred[2048]{0:T(1024)(128)(4,1)}, pred[2048]{0:T(1024)(128)(4,1)S(1)}, u32[]{:S(2)}) copy-start(pred[2048]{0:T(1024)(128)(4,1)S(1)} %compare_and_fusion) | copy-start | bytes 6148
  19.5 15.7 %copy-start = (f32[2,16,1024]{2,1,0:T(8,128)S(1)}, f32[2,16,1024]{2,1,0:T(8,128)}, u32[]{:S(2)}) copy-start(f32[2,16,1024]{2,1,0:T(8,128)} %param.10) | copy-start | bytes 393220
  19.5 15.7 %copy-start.47 = (s32[8,1024]{1,0:T(8,128)S(1)}, s32[8,1024]{1,0:T(8,128)}, u32[]{:S(2)}) copy-start(s32[8,1024]{1,0:T(8,128)} %param.15) | copy-start | bytes 98308
  19.5 15.9 %copy-start.48 = (f32[8,1024]{1,0:T(8,128)S(1)}, f32[8,1024]{1,0:T(8,128)}, u32[]{:S(2)}) copy-start(f32[8,1024]{1,0:T(8,128)} %param.12) | copy-start | bytes 98308
  19.5 15.9 %copy-start.65 = (f32[1024]{0:T(1024)S(1)}, f32[1024]{0:T(1024)}, u32[]{:S(2)}) copy-start(f32[1024]{0:T(1024)} %param.13) | copy-start | bytes 12292
  19.5 29.1 %copy-start.5 = (f32[2,8,1024]{2,1,0:T(8,128)S(1)}, f32[2,8,1024]{2,1,0:T(8,128)}, u32[]{:S(2)}) copy-start(f32[2,8,1024]{2,1,0:T(8,128)} %param.11) | copy-start | bytes 196612
  31.5 40.0 %all-to-all-start = ((f32[2,16,8,256]{3,1,0,2:T(8,128)}), f32[2,16,8,256]{3,1,0,2:T(8,128)S(1)}, u32[]{:S(2)}, u32[]{:S(2)}) async-start(f32[2,16,8,256]{3,1,0,2:T(8,128)} %copy.120), calls=%async_computation | async-start | bytes 524288 | tf_op jit(solution)/shard_map/all_to_all | solution.py:35
  35.3 206.7 %copy-start.21 = (s32[1024]{0:T(1024)}, s32[1024]{0:T(1024)S(1)}, u32[]{:S(2)}) copy-start(s32[1024]{0:T(1024)S(1)} %get-tuple-element.74) | copy-start | bytes 12292
  35.3 212.2 %copy-start.18 = (s32[1024]{0:T(1024)}, s32[1024]{0:T(1024)S(1)}, u32[]{:S(2)}) copy-start(s32[1024]{0:T(1024)S(1)} %get-tuple-element.75) | copy-start | bytes 12292
  35.3 86.6 %copy-start.49 = (pred[1024]{0:T(1024)(128)(4,1)}, pred[1024]{0:T(1024)(128)(4,1)S(1)}, u32[]{:S(2)}) copy-start(pred[1024]{0:T(1024)(128)(4,1)S(1)} %get-tuple-element.76) | copy-start | bytes 3076
  35.3 86.6 %copy-start.51 = (pred[1024]{0:T(1024)(128)(4,1)}, pred[1024]{0:T(1024)(128)(4,1)S(1)}, u32[]{:S(2)}) copy-start(pred[1024]{0:T(1024)(128)(4,1)S(1)} %get-tuple-element.77) | copy-start | bytes 3076
  35.3 187.9 %copy-start.27 = (s32[1024]{0:T(1024)}, s32[1024]{0:T(1024)S(1)}, u32[]{:S(2)}) copy-start(s32[1024]{0:T(1024)S(1)} %get-tuple-element.72) | copy-start | bytes 12292
  35.4 197.3 %copy-start.24 = (s32[1024]{0:T(1024)}, s32[1024]{0:T(1024)S(1)}, u32[]{:S(2)}) copy-start(s32[1024]{0:T(1024)S(1)} %get-tuple-element.73) | copy-start | bytes 12292
  35.4 86.5 %copy-start.53 = (pred[1024]{0:T(1024)(128)(4,1)}, pred[1024]{0:T(1024)(128)(4,1)S(1)}, u32[]{:S(2)}) copy-start(pred[1024]{0:T(1024)(128)(4,1)S(1)} %get-tuple-element.78) | copy-start | bytes 3076
  35.4 86.5 %copy-start.55 = (pred[1024]{0:T(1024)(128)(4,1)}, pred[1024]{0:T(1024)(128)(4,1)S(1)}, u32[]{:S(2)}) copy-start(pred[1024]{0:T(1024)(128)(4,1)S(1)} %get-tuple-element.79) | copy-start | bytes 3076
  35.5 86.5 %copy-start.6 = (f32[1,1024]{1,0:T(1,128)}, f32[1,1024]{1,0:T(1,128)S(1)}, u32[]{:S(2)}) copy-start(f32[1,1024]{1,0:T(1,128)S(1)} %get-tuple-element.31) | copy-start | bytes 12292
  35.5 86.5 %copy-start.8 = (f32[1,1024]{1,0:T(1,128)}, f32[1,1024]{1,0:T(1,128)S(1)}, u32[]{:S(2)}) copy-start(f32[1,1024]{1,0:T(1,128)S(1)} %get-tuple-element.32) | copy-start | bytes 12292
  35.5 86.5 %copy-start.10 = (f32[1,1024]{1,0:T(1,128)}, f32[1,1024]{1,0:T(1,128)S(1)}, u32[]{:S(2)}) copy-start(f32[1,1024]{1,0:T(1,128)S(1)} %get-tuple-element.33) | copy-start | bytes 12292
  35.5 86.5 %copy-start.12 = (f32[1,1024]{1,0:T(1,128)}, f32[1,1024]{1,0:T(1,128)S(1)}, u32[]{:S(2)}) copy-start(f32[1,1024]{1,0:T(1,128)S(1)} %get-tuple-element.34) | copy-start | bytes 12292
  35.5 86.5 %copy-start.14 = (f32[1,1024]{1,0:T(1,128)}, f32[1,1024]{1,0:T(1,128)S(1)}, u32[]{:S(2)}) copy-start(f32[1,1024]{1,0:T(1,128)S(1)} %get-tuple-element.35) | copy-start | bytes 12292
  35.5 86.5 %copy-start.16 = (f32[1,1024]{1,0:T(1,128)}, f32[1,1024]{1,0:T(1,128)S(1)}, u32[]{:S(2)}) copy-start(f32[1,1024]{1,0:T(1,128)S(1)} %get-tuple-element.36) | copy-start | bytes 12292
  36.1 149.6 %copy-start.36 = (s32[1024]{0:T(1024)}, s32[1024]{0:T(1024)S(1)}, u32[]{:S(2)}) copy-start(s32[1024]{0:T(1024)S(1)} %get-tuple-element.68) | copy-start | bytes 12292
  36.1 159.0 %copy-start.30 = (s32[1024]{0:T(1024)}, s32[1024]{0:T(1024)S(1)}, u32[]{:S(2)}) copy-start(s32[1024]{0:T(1024)S(1)} %get-tuple-element.69) | copy-start | bytes 12292
  36.2 168.3 %copy-start.39 = (s32[1024]{0:T(1024)}, s32[1024]{0:T(1024)S(1)}, u32[]{:S(2)}) copy-start(s32[1024]{0:T(1024)S(1)} %get-tuple-element.70) | copy-start | bytes 12292
  36.2 177.7 %copy-start.33 = (s32[1024]{0:T(1024)}, s32[1024]{0:T(1024)S(1)}, u32[]{:S(2)}) copy-start(s32[1024]{0:T(1024)S(1)} %get-tuple-element.71) | copy-start | bytes 12292
  36.2 85.8 %copy-start.57 = (pred[1024]{0:T(1024)(128)(4,1)}, pred[1024]{0:T(1024)(128)(4,1)S(1)}, u32[]{:S(2)}) copy-start(pred[1024]{0:T(1024)(128)(4,1)S(1)} %get-tuple-element.80) | copy-start | bytes 3076
  36.2 85.8 %copy-start.59 = (pred[1024]{0:T(1024)(128)(4,1)}, pred[1024]{0:T(1024)(128)(4,1)S(1)}, u32[]{:S(2)}) copy-start(pred[1024]{0:T(1024)(128)(4,1)S(1)} %get-tuple-element.81) | copy-start | bytes 3076
  36.2 6.3 %collective-permute-start.1 = (f32[2,8,1024]{2,1,0:T(8,128)S(1)}, f32[2,8,1024]{2,1,0:T(8,128)S(1)}, u32[]{:S(2)}, u32[]{:S(2)}) collective-permute-start(f32[2,8,1024]{2,1,0:T(8,128)S(1)} %collective-permute-done), channel_id=1, source_target_pairs={{0,1},{1,2},{2,3},{3,0},{4,5},{5,6},{6,7},{7,4},{8,9},{9,10},{10,1... | collective-permute-start | bytes 196616 | tf_op jit(solution)/shard_map/ppermute | solution.py:22
  37.9 84.1 %copy-start.61 = (pred[1024]{0:T(1024)(128)(4,1)}, pred[1024]{0:T(1024)(128)(4,1)S(1)}, u32[]{:S(2)}) copy-start(pred[1024]{0:T(1024)(128)(4,1)S(1)} %get-tuple-element.82) | copy-start | bytes 3076
  37.9 84.1 %copy-start.63 = (pred[1024]{0:T(1024)(128)(4,1)}, pred[1024]{0:T(1024)(128)(4,1)S(1)}, u32[]{:S(2)}) copy-start(pred[1024]{0:T(1024)(128)(4,1)S(1)} %get-tuple-element.83) | copy-start | bytes 3076
  42.6 6.1 %collective-permute-start.2 = (f32[2,8,1024]{2,1,0:T(8,128)S(1)}, f32[2,8,1024]{2,1,0:T(8,128)S(1)}, u32[]{:S(2)}, u32[]{:S(2)}) collective-permute-start(f32[2,8,1024]{2,1,0:T(8,128)S(1)} %collective-permute-done.1), channel_id=1, source_target_pairs={{0,1},{1,2},{2,3},{3,0},{4,5},{5,6},{6,7},{7,4},{8,9},{9,10},{10,1... | collective-permute-start | bytes 196616 | tf_op jit(solution)/shard_map/ppermute | solution.py:22
  172.1 10.3 %all-to-all-start.1 = ((f32[2,16,8,256]{3,1,0,2:T(8,128)}), f32[2,16,8,256]{3,1,0,2:T(8,128)S(1)}, u32[]{:S(2)}, u32[]{:S(2)}) async-start(f32[2,16,8,256]{3,1,0,2:T(8,128)} %copy.139), calls=%async_computation.1 | async-start | bytes 524288 | tf_op jit(solution)/shard_map/all_to_all | solution.py:35
  264.8 37.8 %copy-start.45 = (pred[2048]{0:T(1024)(128)(4,1)S(1)}, pred[2048]{0:T(1024)(128)(4,1)}, u32[]{:S(2)}) copy-start(pred[2048]{0:T(1024)(128)(4,1)} %copy-done.44) | copy-start | bytes 6148
  314.5 13.7 %copy-start.37 = (s32[1024]{0:T(1024)S(1)}, s32[1024]{0:T(1024)}, u32[]{:S(2)}) copy-start(s32[1024]{0:T(1024)} %copy-done.36) | copy-start | bytes 12292
  314.5 23.1 %copy-start.31 = (s32[1024]{0:T(1024)S(1)}, s32[1024]{0:T(1024)}, u32[]{:S(2)}) copy-start(s32[1024]{0:T(1024)} %copy-done.30) | copy-start | bytes 12292
  314.5 32.5 %copy-start.40 = (s32[1024]{0:T(1024)S(1)}, s32[1024]{0:T(1024)}, u32[]{:S(2)}) copy-start(s32[1024]{0:T(1024)} %copy-done.39) | copy-start | bytes 12292
  314.5 41.9 %copy-start.34 = (s32[1024]{0:T(1024)S(1)}, s32[1024]{0:T(1024)}, u32[]{:S(2)}) copy-start(s32[1024]{0:T(1024)} %copy-done.33) | copy-start | bytes 12292
  314.5 51.2 %copy-start.28 = (s32[1024]{0:T(1024)S(1)}, s32[1024]{0:T(1024)}, u32[]{:S(2)}) copy-start(s32[1024]{0:T(1024)} %copy-done.27) | copy-start | bytes 12292
  314.5 10.3 %all-to-all-start.2 = ((f32[2,16,8,256]{3,1,0,2:T(8,128)}), f32[2,16,8,256]{3,1,0,2:T(8,128)S(1)}, u32[]{:S(2)}, u32[]{:S(2)}) async-start(f32[2,16,8,256]{3,1,0,2:T(8,128)} %copy.158), calls=%async_computation.2 | async-start | bytes 524288 | tf_op jit(solution)/shard_map/all_to_all | solution.py:35
  317.9 57.1 %copy-start.25 = (s32[1024]{0:T(1024)S(1)}, s32[1024]{0:T(1024)}, u32[]{:S(2)}) copy-start(s32[1024]{0:T(1024)} %copy-done.24) | copy-start | bytes 12292
  324.8 59.7 %copy-start.22 = (s32[1024]{0:T(1024)S(1)}, s32[1024]{0:T(1024)}, u32[]{:S(2)}) copy-start(s32[1024]{0:T(1024)} %copy-done.21) | copy-start | bytes 12292
  324.8 65.1 %copy-start.19 = (s32[1024]{0:T(1024)S(1)}, s32[1024]{0:T(1024)}, u32[]{:S(2)}) copy-start(s32[1024]{0:T(1024)} %copy-done.18) | copy-start | bytes 12292
  408.0 37.7 %copy-start.46 = (pred[2048]{0:T(1024)(128)(4,1)S(1)}, pred[2048]{0:T(1024)(128)(4,1)}, u32[]{:S(2)}) copy-start(pred[2048]{0:T(1024)(128)(4,1)} %copy-done.44) | copy-start | bytes 6148
  457.6 13.7 %copy-start.38 = (s32[1024]{0:T(1024)S(1)}, s32[1024]{0:T(1024)}, u32[]{:S(2)}) copy-start(s32[1024]{0:T(1024)} %copy-done.36) | copy-start | bytes 12292
  457.6 19.2 %copy-start.32 = (s32[1024]{0:T(1024)S(1)}, s32[1024]{0:T(1024)}, u32[]{:S(2)}) copy-start(s32[1024]{0:T(1024)} %copy-done.30) | copy-start | bytes 12292
  457.6 24.6 %copy-start.41 = (s32[1024]{0:T(1024)S(1)}, s32[1024]{0:T(1024)}, u32[]{:S(2)}) copy-start(s32[1024]{0:T(1024)} %copy-done.39) | copy-start | bytes 12292
  457.6 34.0 %copy-start.35 = (s32[1024]{0:T(1024)S(1)}, s32[1024]{0:T(1024)}, u32[]{:S(2)}) copy-start(s32[1024]{0:T(1024)} %copy-done.33) | copy-start | bytes 12292
  457.6 43.4 %copy-start.29 = (s32[1024]{0:T(1024)S(1)}, s32[1024]{0:T(1024)}, u32[]{:S(2)}) copy-start(s32[1024]{0:T(1024)} %copy-done.27) | copy-start | bytes 12292
  457.6 10.3 %all-to-all-start.3 = ((f32[2,16,8,256]{3,1,0,2:T(8,128)}), f32[2,16,8,256]{3,1,0,2:T(8,128)S(1)}, u32[]{:S(2)}, u32[]{:S(2)}) async-start(f32[2,16,8,256]{3,1,0,2:T(8,128)} %copy.177), calls=%async_computation.3 | async-start | bytes 524288 | tf_op jit(solution)/shard_map/all_to_all | solution.py:35
  461.2 49.1 %copy-start.26 = (s32[1024]{0:T(1024)S(1)}, s32[1024]{0:T(1024)}, u32[]{:S(2)}) copy-start(s32[1024]{0:T(1024)} %copy-done.24) | copy-start | bytes 12292
  467.9 51.8 %copy-start.23 = (s32[1024]{0:T(1024)S(1)}, s32[1024]{0:T(1024)}, u32[]{:S(2)}) copy-start(s32[1024]{0:T(1024)} %copy-done.21) | copy-start | bytes 12292
  467.9 61.2 %copy-start.20 = (s32[1024]{0:T(1024)S(1)}, s32[1024]{0:T(1024)}, u32[]{:S(2)}) copy-start(s32[1024]{0:T(1024)} %copy-done.18) | copy-start | bytes 12292
  538.9 4.0 copy-start.1
  539.3 4.6 copy-start.2
  540.8 6.5 %copy-start.7 = (f32[1,1024]{1,0:T(1,128)S(1)}, f32[1,1024]{1,0:T(1,128)}, u32[]{:S(2)}) copy-start(f32[1,1024]{1,0:T(1,128)} %copy-done.6) | copy-start | bytes 12292
  540.8 6.5 %copy-start.9 = (f32[1,1024]{1,0:T(1,128)S(1)}, f32[1,1024]{1,0:T(1,128)}, u32[]{:S(2)}) copy-start(f32[1,1024]{1,0:T(1,128)} %copy-done.8) | copy-start | bytes 12292
  543.9 3.4 copy-start.13
  543.9 3.4 copy-start.15
  543.9 3.4 copy-start.17
  543.9 3.4 copy-start.42
  543.9 3.4 copy-start.43
  543.9 3.4 copy-start.50
  544.0 3.4 copy-start.52
  (10 other events, 33.9 us)
